TPU v7x, 32 devices: a whole 2x2x4 slice. The times are simulated.
32 devices in a mesh: var: 16 (over z, y, core), samp: 2 (over x).
Axes of the slice: x: 2, y: 2, z: 4, core: 2. Of those that a mesh axis runs over, the one named last changes fastest.
Arguments:
- genotypes: bfloat16 [4096, 12288], P('samp', 'var'), may hold values from -6 to 6
- marginal: float32 [12288, 1024], P('var', 'samp'), may hold values from -6 to 6
- start_effects: float32 [12288, 1024], P('var', 'samp'), may hold values from -5 to 5
- thresholds: float32 [1024], P('samp'), may hold values from 0.02 to 0.5
Outputs:
- shrunk_effects: float32 [12288, 1024], P('var', 'samp')
All inputs are finite; a program needn't handle non-finite values.
Results may differ from a plain program's by a relative error of at most 0.0003.
Values may be sent and summed in bfloat16 or wider, within the bound.
A program may use at most 64 MiB of HBM per device.

v0:
```python
import jax
import jax.numpy as jnp
from jax import lax
from jax.sharding import PartitionSpec as P

TILE = 256
SWEEPS = 2


shrinkage = 0.2


def with_halo(block, sides, width):
    for axis, dim in sides:
        count = lax.axis_size(axis)
        forward = [(i, i + 1) for i in range(count - 1)]
        backward = [(target, source) for source, target in forward]
        low = lax.ppermute(
            lax.slice_in_dim(block, block.shape[dim] - width, None, axis=dim), axis, forward
        )
        high = lax.ppermute(lax.slice_in_dim(block, 0, width, axis=dim), axis, backward)
        block = jnp.concatenate([low, block, high], axis=dim)
    return block


def gram_tile(left_tile, right_tiles):
    return lax.dot_general(
        left_tile, right_tiles, (((0,), (0,)), ((), ())), preferred_element_type=jnp.float32
    )


def local(genotypes, marginal, start_effects, thresholds):
    sample_count, var_count = genotypes.shape
    sample_total = sample_count * lax.axis_size("samp")
    tile_count = var_count // TILE
    widened = with_halo(genotypes, (("var", 1),), TILE)
    tile_rows = []
    for index in range(tile_count):
        own_tile = widened[:, (index + 1) * TILE : (index + 2) * TILE]
        window = widened[:, index * TILE : (index + 3) * TILE]
        tile_rows.append(gram_tile(own_tile, window))
    ld_band = lax.psum(jnp.stack(tile_rows), "samp") / sample_total
    ld_diagonal = jnp.concatenate(
        [jnp.diagonal(ld_band[index][:, TILE : 2 * TILE]) for index in range(tile_count)]
    )
    divisor = (1.0 - shrinkage) * ld_diagonal + shrinkage
    limit_rows = thresholds[None, :]
    effects = start_effects
    for sweep_index in range(SWEEPS):
        padded = with_halo(effects, (("var", 0),), TILE)
        pieces = []
        for index in range(tile_count):
            pieces.append(
                jnp.dot(
                    ld_band[index],
                    padded[index * TILE : (index + 3) * TILE],
                    precision=lax.Precision.HIGHEST,
                    preferred_element_type=jnp.float32,
                )
            )
        combined = jnp.concatenate(pieces, axis=0)
        cross_term = (1.0 - shrinkage) * (combined - ld_diagonal[:, None] * effects)
        adjusted = marginal - cross_term
        effects = (adjusted - jnp.clip(adjusted, -limit_rows, limit_rows)) / divisor[:, None]
    return effects


def solution(mesh):
    in_specs = (P("samp", "var"), P("var", "samp"), P("var", "samp"), P("samp"))
    out_specs = P("var", "samp")
    return jax.shard_map(local, mesh=mesh, in_specs=in_specs, out_specs=out_specs, check_vma=False)
```

profile of v0, /device:TPU:12, one launch (start us, length us, event | category | flops | bytes accessed | tf_op | source)
XLA Modules:
  0.0 154.9 jit_solution(11081906583868770289)
XLA Ops:
  6.5 0.0 copy-start.3
  6.5 0.0 all-reduce.2.cloned.1.call-start
  6.5 1.8 %fusion.29 = (bf16[2048,256]{1,0:T(8,128)(2,1)S(1)}, bf16[2048,256]{1,0:T(8,128)(2,1)S(1)}) fusion(bf16[2048,768]{1,0:T(8,128)(2,1)} %param.4), kind=kLoop, calls=%fused_computation.53 | loop fusion | bytes 4194304 | tf_op jit(solution)/shard_map/slice | solution.py:19
  8.4 1.9 %collective-permute-start = (bf16[2048,256]{1,0:T(8,128)(2,1)S(1)}, bf16[2048,256]{1,0:T(8,128)(2,1)S(1)}, u32[]{:S(2)}, u32[]{:S(2)}) collective-permute-start(bf16[2048,256]{1,0:T(8,128)(2,1)S(1)} %get-tuple-element.5), channel_id=1, source_target_pairs={{0,2},{2,4},{4,6},{6,8},{8,10},{10,12},{12,14},{14,16},{16,18},{18... | collective-permute-start | bytes 3145736 | tf_op jit(solution)/shard_map/ppermute | solution.py:18
  10.3 3.6 %collective-permute-start.1 = (bf16[2048,256]{1,0:T(8,128)(2,1)S(1)}, bf16[2048,256]{1,0:T(8,128)(2,1)S(1)}, u32[]{:S(2)}, u32[]{:S(2)}) collective-permute-start(bf16[2048,256]{1,0:T(8,128)(2,1)S(1)} %get-tuple-element.6), channel_id=1, source_target_pairs={{2,0},{4,2},{6,4},{8,6},{10,8},{12,10},{14,12},{16,14},{18,16},{20... | collective-permute-start | bytes 3145736 | tf_op jit(solution)/shard_map/ppermute | solution.py:21
  14.0 0.0 copy-done.3
  14.0 1.3 convolution_bitcast_fusion
  15.3 20.4 %collective-permute-done = bf16[2048,256]{1,0:T(8,128)(2,1)S(1)} collective-permute-done((bf16[2048,256]{1,0:T(8,128)(2,1)S(1)}, bf16[2048,256]{1,0:T(8,128)(2,1)S(1)}, u32[]{:S(2)}, u32[]{:S(2)}) %collective-permute-start) | collective-permute-done | bytes 1048608 | tf_op jit(solution)/shard_map/ppermute | solution.py:18
  35.7 1.0 fusion.16
  36.8 0.0 collective-permute-done.1
  36.8 1.0 fusion.17
  37.8 1.6 %pad_maximum_fusion.4 = f32[3,256,768]{1,2,0:T(8,128)} fusion(f32[1,256,768]{1,2,0:T(8,128)S(1)} %fusion.17, f32[1,256,768]{1,2,0:T(8,128)S(1)} %convolution_bitcast_fusion, f32[1,256,768]{1,2,0:T(8,128)S(1)} %fusion.16), kind=kLoop, calls=%fused_computation.9 | loop fusion | flops 1179648 | bytes 4718592 | tf_op jit(solution)/shard_map/stack | solution.py:42
  39.4 0.0 copy-start
  39.4 0.0 all-reduce.2.cloned.1.call-update
  39.4 1.4 copy-done
  40.8 0.0 copy-start.4
  40.8 0.9 fusion.31
  41.7 1.9 %collective-permute-start.2 = (f32[256,512]{1,0:T(8,128)}, f32[256,512]{1,0:T(8,128)}, u32[]{:S(2)}, u32[]{:S(2)}) collective-permute-start(f32[256,512]{1,0:T(8,128)} %get-tuple-element.12), channel_id=1, source_target_pairs={{0,2},{2,4},{4,6},{6,8},{8,10},{10,12},{12,14},{14,16},{16,18},{18... | collective-permute-start | bytes 1572872 | tf_op jit(solution)/shard_map/ppermute | solution.py:18
  43.6 3.6 %collective-permute-start.3 = (f32[256,512]{1,0:T(8,128)S(1)}, f32[256,512]{1,0:T(8,128)}, u32[]{:S(2)}, u32[]{:S(2)}) collective-permute-start(f32[256,512]{1,0:T(8,128)S(1)} %get-tuple-element.13), channel_id=1, source_target_pairs={{2,0},{4,2},{6,4},{8,6},{10,8},{12,10},{14,12},{16,14},{18,16},{20... | collective-permute-start | bytes 1572872 | tf_op jit(solution)/shard_map/ppermute | solution.py:21
  47.2 0.0 copy-done.4
  47.3 61.1 %all-reduce.2.cloned.1.call-done = f32[3,256,768]{1,2,0:T(8,128)} async-done(((f32[3,256,768]{1,2,0:T(8,128)}), f32[3,256,768]{1,2,0:T(8,128)}) %all-reduce.2.cloned.1.call-update) | async-done | bytes 2359312 | tf_op jit(solution)/shard_map/psum | solution.py:42
  108.3 1.8 %broadcast_multiply_fusion = f32[3,256,768]{1,2,0:T(8,128)S(1)} fusion(f32[3,256,768]{1,2,0:T(8,128)} %all-reduce.2.cloned.1.call-done), kind=kLoop, calls=%fused_computation.33 | loop fusion | flops 589824 | bytes 4718592 | tf_op jit(solution)/shard_map/div | solution.py:42
  110.2 1.0 slice_bitcast_fusion
  111.2 2.4 %gather_fusion = f32[256]{0:T(256)S(1)} fusion(f32[256,256]{0,1:T(8,128)S(1)} %slice.99, s32[256]{0:T(256)S(1)} %bitcast.26), kind=kCustom, calls=%fused_computation | custom fusion | bytes 4096 | tf_op jit(solution)/shard_map/jit(diagonal)/cond/branch_0_fun/gather | solution.py:44
  113.6 2.4 %gather_fusion.1 = f32[256]{0:T(256)S(1)} fusion(f32[256,256]{0,1:T(8,128)S(1)} %slice.100, s32[256]{0:T(256)S(1)} %bitcast.27), kind=kCustom, calls=%fused_computation.1 | custom fusion | bytes 4096 | tf_op jit(solution)/shard_map/jit(diagonal)/cond/branch_0_fun/gather | solution.py:44
  116.0 1.0 slice.101
  117.0 2.4 %gather_fusion.2 = f32[256]{0:T(256)S(1)} fusion(f32[256,256]{0,1:T(8,128)S(1)} %slice.101, s32[256]{0:T(256)S(1)} %bitcast.28), kind=kCustom, calls=%fused_computation.2 | custom fusion | bytes 4096 | tf_op jit(solution)/shard_map/jit(diagonal)/cond/branch_0_fun/gather | solution.py:44
  119.4 0.0 copy-start.1
  119.4 0.0 collective-permute-done.2
  119.4 3.0 %fusion.10 = f32[256,512]{1,0:T(8,128)S(1)} fusion(f32[768,512]{1,0:T(8,128)} %param.6, f32[256,512]{1,0:T(8,128)} %collective-permute-done.2, f32[3,256,768]{1,2,0:T(8,128)S(1)} %broadcast_multiply_fusion), kind=kOutput, calls=%fused_computation.20 | convolution fusion | flops 1208352768 | bytes 3407872 | tf_op jit(solution)/shard_map/dot_general | solution.py:54
  122.4 0.0 copy-done.1
  122.4 1.5 fusion.26
  123.9 0.0 copy-start.2
  123.9 0.0 collective-permute-done.3
  123.9 2.6 %fusion.8 = f32[256,512]{1,0:T(8,128)S(1)} fusion(f32[256,512]{1,0:T(8,128)} %collective-permute-done.3, f32[768,512]{1,0:T(8,128)S(1)} %copy-done.1, f32[3,256,768]{1,2,0:T(8,128)S(1)} %broadcast_multiply_fusion), kind=kOutput, calls=%fused_computation.17 | convolution fusion | flops 1208352768 | bytes 3407872 | tf_op jit(solution)/shard_map/dot_general | solution.py:54
  126.6 0.0 copy-done.2
  126.6 0.5 subtract_divide_fusion.1
  127.1 0.1 fusion.30
  127.2 1.9 %collective-permute-start.4 = (f32[256,512]{1,0:T(8,128)S(1)}, f32[256,512]{1,0:T(8,128)S(1)}, u32[]{:S(2)}, u32[]{:S(2)}) collective-permute-start(f32[256,512]{1,0:T(8,128)S(1)} %get-tuple-element.10), channel_id=1, source_target_pairs={{0,2},{2,4},{4,6},{6,8},{8,10},{10,12},{12,14},{14,16},{16,18},{18... | collective-permute-start | bytes 1572872 | tf_op jit(solution)/shard_map/ppermute | solution.py:18
  129.1 3.8 %collective-permute-start.5 = (f32[256,512]{1,0:T(8,128)S(1)}, f32[256,512]{1,0:T(8,128)S(1)}, u32[]{:S(2)}, u32[]{:S(2)}) collective-permute-start(f32[256,512]{1,0:T(8,128)S(1)} %get-tuple-element.11), channel_id=1, source_target_pairs={{2,0},{4,2},{6,4},{8,6},{10,8},{12,10},{14,12},{16,14},{18,16},{20... | collective-permute-start | bytes 1572872 | tf_op jit(solution)/shard_map/ppermute | solution.py:21
  133.0 1.5 fusion.25
  134.5 8.8 %collective-permute-done.4 = f32[256,512]{1,0:T(8,128)S(1)} collective-permute-done((f32[256,512]{1,0:T(8,128)S(1)}, f32[256,512]{1,0:T(8,128)S(1)}, u32[]{:S(2)}, u32[]{:S(2)}) %collective-permute-start.4) | collective-permute-done | bytes 524320 | tf_op jit(solution)/shard_map/ppermute | solution.py:18
  143.3 1.5 fusion.6
  144.8 0.0 collective-permute-done.5
  144.8 1.5 fusion.4
  146.4 1.6 %subtract_divide_fusion = f32[768,512]{1,0:T(8,128)} fusion(f32[768,512]{1,0:T(8,128)S(1)} %copy-done.2, f32[256,512]{1,0:T(8,128)S(1)} %fusion.4, f32[256,512]{1,0:T(8,128)S(1)} %fusion.25, f32[256,512]{1,0:T(8,128)S(1)} %fusion.6, f32[768,512]{1,0:T(8,128)S(1)} %subtract_divide_fusion.1, f32[768]{0:T(1024)S(1)} %multiply_add_fusion, f32[512]{0:T(512)S(1)} %neg.5, ...), kind=kLoop, calls=%fused_computation.28 | loop fusion | flops 3932160 | bytes 6301696 | tf_op jit(solution)/shard_map/div | solution.py:64
  (9 shorter events, 0.1 us)
Async XLA Ops:
  6.5 7.4 %copy-start.3 = (bf16[2048,768]{1,0:T(8,128)(2,1)S(1)}, bf16[2048,768]{1,0:T(8,128)(2,1)}, u32[]{:S(2)}) copy-start(bf16[2048,768]{1,0:T(8,128)(2,1)} %param.4) | copy-start | bytes 9437188
  6.5 101.8 %all-reduce.2.cloned.1.call-start = ((), (), s32[]{:S(2)}) async-start(), calls=%async_computation | async-start | bytes 4718592 | tf_op jit(solution)/shard_map/psum | solution.py:42
  8.4 27.4 %collective-permute-start = (bf16[2048,256]{1,0:T(8,128)(2,1)S(1)}, bf16[2048,256]{1,0:T(8,128)(2,1)S(1)}, u32[]{:S(2)}, u32[]{:S(2)}) collective-permute-start(bf16[2048,256]{1,0:T(8,128)(2,1)S(1)} %get-tuple-element.5), channel_id=1, source_target_pairs={{0,2},{2,4},{4,6},{6,8},{8,10},{10,12},{12,14},{14,16},{16,18},{18... | collective-permute-start | bytes 3145736 | tf_op jit(solution)/shard_map/ppermute | solution.py:18
  10.3 26.5 %collective-permute-start.1 = (bf16[2048,256]{1,0:T(8,128)(2,1)S(1)}, bf16[2048,256]{1,0:T(8,128)(2,1)S(1)}, u32[]{:S(2)}, u32[]{:S(2)}) collective-permute-start(bf16[2048,256]{1,0:T(8,128)(2,1)S(1)} %get-tuple-element.6), channel_id=1, source_target_pairs={{2,0},{4,2},{6,4},{8,6},{10,8},{12,10},{14,12},{16,14},{18,16},{20... | collective-permute-start | bytes 3145736 | tf_op jit(solution)/shard_map/ppermute | solution.py:21
  39.4 1.4 copy-start
  40.8 6.5 %copy-start.4 = (f32[512]{0:T(512)S(1)}, f32[512]{0:T(512)}, u32[]{:S(2)}) copy-start(f32[512]{0:T(512)} %param.7) | copy-start | bytes 6148
  41.7 77.7 %collective-permute-start.2 = (f32[256,512]{1,0:T(8,128)}, f32[256,512]{1,0:T(8,128)}, u32[]{:S(2)}, u32[]{:S(2)}) collective-permute-start(f32[256,512]{1,0:T(8,128)} %get-tuple-element.12), channel_id=1, source_target_pairs={{0,2},{2,4},{4,6},{6,8},{8,10},{10,12},{12,14},{14,16},{16,18},{18... | collective-permute-start | bytes 1572872 | tf_op jit(solution)/shard_map/ppermute | solution.py:18
  43.6 80.4 %collective-permute-start.3 = (f32[256,512]{1,0:T(8,128)S(1)}, f32[256,512]{1,0:T(8,128)}, u32[]{:S(2)}, u32[]{:S(2)}) collective-permute-start(f32[256,512]{1,0:T(8,128)S(1)} %get-tuple-element.13), channel_id=1, source_target_pairs={{2,0},{4,2},{6,4},{8,6},{10,8},{12,10},{14,12},{16,14},{18,16},{20... | collective-permute-start | bytes 1572872 | tf_op jit(solution)/shard_map/ppermute | solution.py:21
  119.4 3.0 %copy-start.1 = (f32[768,512]{1,0:T(8,128)S(1)}, f32[768,512]{1,0:T(8,128)}, u32[]{:S(2)}) copy-start(f32[768,512]{1,0:T(8,128)} %param.6) | copy-start | bytes 4718596
  123.9 2.7 %copy-start.2 = (f32[768,512]{1,0:T(8,128)S(1)}, f32[768,512]{1,0:T(8,128)}, u32[]{:S(2)}) copy-start(f32[768,512]{1,0:T(8,128)} %param.5) | copy-start | bytes 4718596
  127.2 16.1 %collective-permute-start.4 = (f32[256,512]{1,0:T(8,128)S(1)}, f32[256,512]{1,0:T(8,128)S(1)}, u32[]{:S(2)}, u32[]{:S(2)}) collective-permute-start(f32[256,512]{1,0:T(8,128)S(1)} %get-tuple-element.10), channel_id=1, source_target_pairs={{0,2},{2,4},{4,6},{6,8},{8,10},{10,12},{12,14},{14,16},{16,18},{18... | collective-permute-start | bytes 1572872 | tf_op jit(solution)/shard_map/ppermute | solution.py:18
  129.1 15.7 %collective-permute-start.5 = (f32[256,512]{1,0:T(8,128)S(1)}, f32[256,512]{1,0:T(8,128)S(1)}, u32[]{:S(2)}, u32[]{:S(2)}) collective-permute-start(f32[256,512]{1,0:T(8,128)S(1)} %get-tuple-element.11), channel_id=1, source_target_pairs={{2,0},{4,2},{6,4},{8,6},{10,8},{12,10},{14,12},{16,14},{18,16},{20... | collective-permute-start | bytes 1572872 | tf_op jit(solution)/shard_map/ppermute | solution.py:21
Sparse Core Ops, SparseCore 0:
  39.5 68.7 all-reduce.1
where the time goes:
time: 155 us
  waiting for transfers between devices  90.4 us (58%)
  starting transfers between devices  16.9 us (11%)
  matrix products  15 us (10%)
  between operations  13.7 us (9%)
  local copies, waits for them, and re-layouts  13.4 us (9%)
  other arithmetic  5.58 us (4%)
    psum x1, waiting for transfers between devices, local(): ld_band = lax.psum(jnp.stack(tile_rows), 'samp') / sample_total  61.1 us
    ppermute x3, waiting for transfers between devices, with_halo(): lax.ppermute(lax.slice_in_dim(block, block.shape[dim] - width, None, axis...  29.3 us
    dot_general x6, matrix products, local(): jnp.dot(ld_band[index], padded[index * TILE:(index + 3) * TILE], precisio...  11.6 us
    ppermute x3, starting transfers between devices, with_halo(): lax.ppermute(lax.slice_in_dim(block, 0, width, axis=dim), axis, backward)  11.1 us
    gather x3, local copies, waits for them, and re-layouts, local(): jnp.diagonal(ld_band[index][:, TILE:2 * TILE])  7.11 us
    ppermute x3, starting transfers between devices, with_halo(): lax.ppermute(lax.slice_in_dim(block, block.shape[dim] - width, None, axis...  5.75 us
    dot_general x3, matrix products, gram_tile(): lax.dot_general(left_tile, right_tiles, (((0,), (0,)), ((), ())), preferr...  3.37 us
  transfers between devices with their start and end apart: 7, of which 3 were waited for; matrix products, arithmetic and copies ran while one was open for 14% of the time, Pallas kernels for 0%

commit v1 on v0

v1 whole, which is shorter than its diff:
```python
import functools

import jax
import jax.numpy as jnp
from jax import lax
from jax.experimental import pallas as pl
from jax.experimental.pallas import tpu as pltpu
from jax.sharding import PartitionSpec as P

TILE = 256
HALF = TILE // 2
SWEEPS = 2
LD_SCALE = 1024.0

shrinkage = 0.2
MESH = pl.DeviceIdType.MESH
F32 = jnp.float32
BF16 = jnp.bfloat16


def encode(value):
    square = value * value
    fourth = square * square
    eighth = fourth * fourth
    return jnp.where(value < 0, -eighth, eighth).astype(BF16)


def decode(code):
    code = code.astype(F32)
    root = jnp.sqrt(jnp.sqrt(jnp.sqrt(jnp.abs(code))))
    return jnp.where(code < 0, -root, root)


def split(value):
    high = value.astype(BF16)
    return high, (value - high.astype(F32)).astype(BF16)


def iota_pair(size):
    row = lax.broadcasted_iota(jnp.int32, (size, size), 0)
    col = lax.broadcasted_iota(jnp.int32, (size, size), 1)
    return row, col


def pack_symmetric(tile):
    row, col = iota_pair(HALF)
    mixed = jnp.where(row < col, tile[:HALF, :HALF], tile[HALF:, HALF:])
    return jnp.concatenate([mixed, tile[:HALF, HALF:]], axis=1)


def unpack_symmetric(packed):
    row, col = iota_pair(HALF)
    mixed, corner = packed[:, :HALF], packed[:, HALF:]
    upper = jnp.where(row < col, mixed, 0.0)
    lower = jnp.where(row > col, mixed, 0.0)
    first = jnp.concatenate([upper + upper.T, corner], axis=1)
    second = jnp.concatenate([corner.T, lower + lower.T], axis=1)
    return jnp.concatenate([first, second], axis=0)


def gram(left, right):
    return lax.dot_general(left, right, (((0,), (0,)), ((), ())), preferred_element_type=F32)


def kernel(
    tiles, var_size, samp_size, inv_total,
    geno_hbm, marg_hbm, start_hbm, limit_ref, out_hbm,
    geno, halo, marg, start, own, code, got, diag, diag_got,
    band_hi, band_lo, eff_hi, eff_lo, edge_code, edge_got, cross_code, cross_got, result,
    load_sem, store_sem, geno_sem, part_send, part_recv, cross_sem, edge_send, edge_recv,
):
    var = lax.axis_index("var")
    samp = lax.axis_index("samp")
    has_prev = var > 0
    has_next = var < var_size - 1
    prev, following = var - 1, var + 1
    peers = [lax.rem(samp + k, samp_size) for k in range(1, samp_size)]
    last = tiles - 1
    columns = geno.shape[1]

    step = HALF + TILE
    cross_at = tiles * step - TILE
    total_rows = cross_at + TILE

    loads = []
    for t in range(tiles):
        cols = pl.ds(t * TILE, TILE)
        loads.append(pltpu.make_async_copy(geno_hbm.at[:, cols], geno.at[:, cols], load_sem.at[t]))
    loads.append(pltpu.make_async_copy(start_hbm, start, load_sem.at[tiles]))
    loads.append(pltpu.make_async_copy(marg_hbm, marg, load_sem.at[tiles + 1]))
    for copy in loads:
        copy.start()

    barrier = pltpu.get_barrier_semaphore()

    @pl.when(has_prev)
    def _():
        pl.semaphore_signal(barrier, inc=1, device_id={"var": prev}, device_id_type=MESH)

    @pl.when(has_next)
    def _():
        pl.semaphore_signal(barrier, inc=1, device_id={"var": following}, device_id_type=MESH)

    for peer in peers:
        pl.semaphore_signal(barrier, inc=1, device_id={"samp": peer}, device_id_type=MESH)
    pl.semaphore_wait(
        barrier, len(peers) + has_prev.astype(jnp.int32) + has_next.astype(jnp.int32)
    )

    geno_copy = pltpu.make_async_remote_copy(
        src_ref=geno_hbm.at[:, pl.ds(last * TILE, TILE)], dst_ref=halo,
        send_sem=geno_sem.at[0], recv_sem=geno_sem.at[1],
        device_id={"var": following}, device_id_type=MESH,
    )

    @pl.when(has_next)
    def _():
        geno_copy.start()

    def part_copy(k, message):
        if message == tiles + 1:
            src, dst = diag, diag_got.at[k]
        else:
            begin = message * step if message < tiles else cross_at
            rows = pl.ds(begin, TILE if message == tiles else HALF if message == last else step)
            src, dst = code.at[rows], got.at[k, rows]
        return pltpu.make_async_remote_copy(
            src_ref=src, dst_ref=dst,
            send_sem=part_send.at[k, message], recv_sem=part_recv.at[k, message],
            device_id={"samp": peers[k]}, device_id_type=MESH,
        )

    def send_part(message):
        for k in range(len(peers)):
            part_copy(k, message).start()

    diag[...] = jnp.zeros_like(diag)
    row, col = iota_pair(TILE)
    on_diagonal = row == col

    for t in range(tiles):
        if t == 0:
            loads[0].wait()
        if t + 1 < tiles:
            loads[t + 1].wait()
        width = min(2, tiles - t) * TILE
        product = gram(geno[:, t * TILE : (t + 1) * TILE], geno[:, t * TILE : t * TILE + width])
        product = product * (inv_total * LD_SCALE)
        block = product[:, :TILE]
        diag[pl.ds(t, 1), :] = jnp.sum(jnp.where(on_diagonal, block, 0.0), axis=0, keepdims=True)
        begin = t * step
        packed = pack_symmetric(block)
        own[begin : begin + HALF] = packed
        code[begin : begin + HALF] = encode(packed)
        if t + 1 < tiles:
            beside = product[:, TILE:]
            own[begin + HALF : begin + step] = beside
            code[begin + HALF : begin + step] = encode(beside)
        send_part(t)
    send_part(tiles + 1)

    loads[tiles].wait()
    loads[tiles + 1].wait()

    def place(sweep, slot, value):
        high, low = split(value)
        eff_hi[sweep, slot * TILE : (slot + 1) * TILE] = high
        eff_lo[sweep, slot * TILE : (slot + 1) * TILE] = low

    def clear(sweep, slot):
        zero = jnp.zeros((TILE, eff_hi.shape[2]), BF16)
        eff_hi[sweep, slot * TILE : (slot + 1) * TILE] = zero
        eff_lo[sweep, slot * TILE : (slot + 1) * TILE] = zero

    for t in range(tiles):
        place(0, t + 1, start[t * TILE : (t + 1) * TILE])
    edge_code[0, 0] = encode(start[:TILE])
    edge_code[0, 1] = encode(start[last * TILE :])

    def edge_copy(sweep, side):
        return pltpu.make_async_remote_copy(
            src_ref=edge_code.at[sweep, side], dst_ref=edge_got.at[sweep, side],
            send_sem=edge_send.at[sweep, side], recv_sem=edge_recv.at[sweep, side],
            device_id={"var": following if side else prev}, device_id_type=MESH,
        )

    def send_edge(sweep, side):
        @pl.when(has_next if side else has_prev)
        def _():
            edge_copy(sweep, side).start()

    def take_edge(sweep, side):
        slot = 0 if side else tiles + 1
        exists = has_prev if side else has_next

        @pl.when(exists)
        def _():
            edge_copy(sweep, side).wait_recv()
            place(sweep, slot, decode(edge_got[sweep, side]))

        @pl.when(jnp.logical_not(exists))
        def _():
            clear(sweep, slot)

    @pl.when(has_prev)
    def _():
        geno_copy.wait_recv()
        product = gram(halo[...], geno[:, :TILE]) * (inv_total * LD_SCALE)
        own[cross_at:total_rows] = product
        code[cross_at:total_rows] = encode(product)
        send_part(tiles)

    send_edge(0, 1)
    send_edge(0, 0)

    def summed(begin, size):
        value = own[begin : begin + size]
        for k in range(len(peers)):
            value = value + decode(got[k, begin : begin + size])
        return value

    def put(tile, slot, value):
        high, low = split(value)
        band_hi[tile, :, slot * TILE : (slot + 1) * TILE] = high
        band_lo[tile, :, slot * TILE : (slot + 1) * TILE] = low

    for k in range(len(peers)):
        part_copy(k, tiles + 1).wait_recv()
    for t in range(tiles):
        for k in range(len(peers)):
            part_copy(k, t).wait_recv()
        begin = t * step
        put(t, 1, unpack_symmetric(summed(begin, HALF)) * (1.0 / LD_SCALE))
        if t + 1 < tiles:
            beside = summed(begin + HALF, TILE) * (1.0 / LD_SCALE)
            put(t, 2, beside)
            put(t + 1, 0, beside.T)

    keep = []
    for t in range(tiles):
        whole = diag[pl.ds(t, 1), :]
        for k in range(len(peers)):
            whole = whole + diag_got[k, pl.ds(t, 1), :]
        column = jnp.sum(jnp.where(on_diagonal, whole, 0.0), axis=1, keepdims=True) * (1.0 / LD_SCALE)
        keep.append(1.0 / ((1.0 - shrinkage) * column + shrinkage))
    limit = limit_ref[...]

    def applied(sweep, tile, first, count):
        cols = slice(first * TILE, (first + count) * TILE)
        rows = slice((tile + first) * TILE, (tile + first + count) * TILE)
        high, low = band_hi[tile, :, cols], band_lo[tile, :, cols]
        near, rest = eff_hi[sweep, rows], eff_lo[sweep, rows]
        dot = functools.partial(jnp.dot, preferred_element_type=F32)
        return dot(high, near) + (dot(high, rest) + dot(low, near))

    def finish(tile, combined):
        adjusted = marg[tile * TILE : (tile + 1) * TILE] - (1.0 - shrinkage) * combined
        shrunk = adjusted - jnp.clip(adjusted, -limit, limit)
        return shrunk * keep[tile]

    for t in range(1, tiles - 1):
        place(1, t + 1, finish(t, applied(0, t, 0, 3)))

    def back_copy():
        return pltpu.make_async_remote_copy(
            src_ref=cross_code, dst_ref=cross_got,
            send_sem=cross_sem.at[0], recv_sem=cross_sem.at[1],
            device_id={"var": prev}, device_id_type=MESH,
        )

    @pl.when(has_prev)
    def _():
        for k in range(len(peers)):
            part_copy(k, tiles).wait_recv()
        crossing = summed(cross_at, TILE)
        cross_code[...] = encode(crossing)
        back_copy().start()
        put(0, 0, crossing.T * (1.0 / LD_SCALE))

    @pl.when(jnp.logical_not(has_prev))
    def _():
        put(0, 0, jnp.zeros((TILE, TILE), F32))

    take_edge(0, 1)
    value = finish(0, applied(0, 0, 0, 3))
    edge_code[1, 0] = encode(value)
    send_edge(1, 0)
    place(1, 1, value)

    @pl.when(has_next)
    def _():
        back_copy().wait_recv()
        put(last, 2, decode(cross_got[...]) * (1.0 / LD_SCALE))

    @pl.when(jnp.logical_not(has_next))
    def _():
        put(last, 2, jnp.zeros((TILE, TILE), F32))

    take_edge(0, 0)
    value = finish(last, applied(0, last, 0, 3))
    edge_code[1, 1] = encode(value)
    send_edge(1, 1)
    place(1, tiles, value)

    stores = []

    def emit(tile, combined):
        rows = pl.ds(tile * TILE, TILE)
        result[tile * TILE : (tile + 1) * TILE] = finish(tile, combined)
        copy = pltpu.make_async_copy(result.at[rows], out_hbm.at[rows], store_sem.at[tile])
        copy.start()
        stores.append(copy)

    for t in range(1, tiles - 1):
        emit(t, applied(1, t, 0, 3))
    part = applied(1, last, 0, 2)
    other = applied(1, 0, 1, 2)
    take_edge(1, 0)
    emit(last, part + applied(1, last, 2, 1))
    take_edge(1, 1)
    emit(0, other + applied(1, 0, 0, 1))

    for copy in stores:
        copy.wait()
    for k in range(len(peers)):
        for message in list(range(tiles)) + [tiles + 1]:
            part_copy(k, message).wait_send()

    @pl.when(has_prev)
    def _():
        for k in range(len(peers)):
            part_copy(k, tiles).wait_send()
        back_copy().wait_send()
        for sweep in range(SWEEPS):
            edge_copy(sweep, 0).wait_send()

    @pl.when(has_next)
    def _():
        geno_copy.wait_send()
        for sweep in range(SWEEPS):
            edge_copy(sweep, 1).wait_send()


def local(genotypes, marginal, start_effects, thresholds):
    samples, variants = genotypes.shape
    traits = marginal.shape[1]
    tiles = variants // TILE
    var_size, samp_size = lax.axis_size("var"), lax.axis_size("samp")
    others = samp_size - 1
    rows = tiles * (HALF + TILE)
    dma = pltpu.SemaphoreType.DMA
    body = functools.partial(
        kernel, tiles, var_size, samp_size, 1.0 / (samples * samp_size)
    )
    return pl.pallas_call(
        body,
        out_shape=jax.ShapeDtypeStruct((variants, traits), F32),
        in_specs=[pl.BlockSpec(memory_space=pl.ANY)] * 3 + [pl.BlockSpec(memory_space=pltpu.VMEM)],
        out_specs=pl.BlockSpec(memory_space=pl.ANY),
        scratch_shapes=[
            pltpu.VMEM((samples, variants), BF16),
            pltpu.VMEM((samples, TILE), BF16),
            pltpu.VMEM((variants, traits), F32),
            pltpu.VMEM((variants, traits), F32),
            pltpu.VMEM((rows, TILE), F32),
            pltpu.VMEM((rows, TILE), BF16),
            pltpu.VMEM((others, rows, TILE), BF16),
            pltpu.VMEM((8, TILE), F32),
            pltpu.VMEM((others, 8, TILE), F32),
            pltpu.VMEM((tiles, TILE, 3 * TILE), BF16),
            pltpu.VMEM((tiles, TILE, 3 * TILE), BF16),
            pltpu.VMEM((SWEEPS, (tiles + 2) * TILE, traits), BF16),
            pltpu.VMEM((SWEEPS, (tiles + 2) * TILE, traits), BF16),
            pltpu.VMEM((SWEEPS, 2, TILE, traits), BF16),
            pltpu.VMEM((SWEEPS, 2, TILE, traits), BF16),
            pltpu.VMEM((TILE, TILE), BF16),
            pltpu.VMEM((TILE, TILE), BF16),
            pltpu.VMEM((variants, traits), F32),
            dma((tiles + 2,)),
            dma((tiles,)),
            dma((2,)),
            dma((others, tiles + 2)),
            dma((others, tiles + 2)),
            dma((2,)),
            dma((SWEEPS, 2)),
            dma((SWEEPS, 2)),
        ],
        compiler_params=pltpu.CompilerParams(
            collective_id=0, has_side_effects=True, vmem_limit_bytes=60 * 1024 * 1024
        ),
    )(genotypes, marginal, start_effects, thresholds[None, :])


def solution(mesh):
    in_specs = (P("samp", "var"), P("var", "samp"), P("var", "samp"), P("samp"))
    out_specs = P("var", "samp")
    return jax.shard_map(local, mesh=mesh, in_specs=in_specs, out_specs=out_specs, check_vma=False)
```

time: 155 us -> 37.2 us (0.24)
  the two profiles are of different devices: /device:TPU:12 before, /device:TPU:8 now
where the time goes in v1:
time: 37.2 us; the launch traced here: 37 us
  Pallas kernels  34.3 us (92%)
  local copies, waits for them, and re-layouts  2.67 us (7%)
    pallas_call x1, Pallas kernels, local(): pl.pallas_call(body, out_shape=jax.ShapeDtypeStruct((variants, traits), F...  34.3 us
    unnamed x1, local copies, waits for them, and re-layouts  2.67 us

profile of v1, /device:TPU:8, one launch (start us, length us, event | category | flops | bytes accessed | tf_op | source)
XLA Modules:
  0.0 37.0 jit_solution(13711177801926842165)
XLA Ops:
  0.0 34.3 %shard_map.46 = f32[768,512]{1,0:T(8,128)} custom-call(bf16[2048,768]{1,0:T(8,128)(2,1)} %geno_hbm.1, f32[768,512]{1,0:T(8,128)} %marg_hbm.1, f32[768,512]{1,0:T(8,128)} %start_hbm.1, f32[1,512]{1,0:T(1,128)} %bitcast.1), custom_call_target="tpu_custom_call" | custom-call | tf_op jit(solution)/shard_map/pallas_call | solution.py:355
  34.3 2.7 %copy.6 = f32[768,512]{1,0:T(8,128)} copy(f32[768,512]{1,0:T(8,128)} %shard_map.46) | data formatting | bytes 3145728

commit v2 on v1

--- a/solution.py
+++ b/solution.py
@@ -10,6 +10,8 @@
 TILE = 256
 HALF = TILE // 2
 SWEEPS = 2
+CHUNKS = 4
+VMEM_BYTES = 40 * 1024 * 1024
 LD_SCALE = 1024.0
 
 shrinkage = 0.2
@@ -64,10 +66,10 @@
 
 def kernel(
     tiles, var_size, samp_size, inv_total,
-    geno_hbm, marg_hbm, start_hbm, limit_ref, out_hbm,
-    geno, halo, marg, start, own, code, got, diag, diag_got,
-    band_hi, band_lo, eff_hi, eff_lo, edge_code, edge_got, cross_code, cross_got, result,
-    load_sem, store_sem, geno_sem, part_send, part_recv, cross_sem, edge_send, edge_recv,
+    geno_hbm, marg_hbm, start_hbm, limit_hbm, out,
+    geno, halo, marg, start, limit_row, own, code, got, diag, diag_got,
+    band_hi, band_lo, eff_hi, eff_lo, edge_code, edge_got, cross_code, cross_got,
+    load_sem, geno_send, geno_recv, part_send, part_recv, cross_sem, edge_send, edge_recv,
 ):
     var = lax.axis_index("var")
     samp = lax.axis_index("samp")
@@ -76,7 +78,8 @@
     prev, following = var - 1, var + 1
     peers = [lax.rem(samp + k, samp_size) for k in range(1, samp_size)]
     last = tiles - 1
-    columns = geno.shape[1]
+    pieces, width = edge_code.shape[2], edge_code.shape[4]
+    slices = [slice(c * width, (c + 1) * width) for c in range(pieces)]
 
     step = HALF + TILE
     cross_at = tiles * step - TILE
@@ -88,6 +91,7 @@
         loads.append(pltpu.make_async_copy(geno_hbm.at[:, cols], geno.at[:, cols], load_sem.at[t]))
     loads.append(pltpu.make_async_copy(start_hbm, start, load_sem.at[tiles]))
     loads.append(pltpu.make_async_copy(marg_hbm, marg, load_sem.at[tiles + 1]))
+    loads.append(pltpu.make_async_copy(limit_hbm, limit_row, load_sem.at[tiles + 2]))
     for copy in loads:
         copy.start()
 
@@ -107,15 +111,20 @@
         barrier, len(peers) + has_prev.astype(jnp.int32) + has_next.astype(jnp.int32)
     )
 
-    geno_copy = pltpu.make_async_remote_copy(
-        src_ref=geno_hbm.at[:, pl.ds(last * TILE, TILE)], dst_ref=halo,
-        send_sem=geno_sem.at[0], recv_sem=geno_sem.at[1],
-        device_id={"var": following}, device_id_type=MESH,
-    )
+    depth = geno.shape[0] // CHUNKS
+
+    def geno_copy(chunk):
+        rows = pl.ds(chunk * depth, depth)
+        return pltpu.make_async_remote_copy(
+            src_ref=geno_hbm.at[rows, pl.ds(last * TILE, TILE)], dst_ref=halo.at[rows],
+            send_sem=geno_send.at[chunk], recv_sem=geno_recv.at[chunk],
+            device_id={"var": following}, device_id_type=MESH,
+        )
 
     @pl.when(has_next)
     def _():
-        geno_copy.start()
+        for chunk in range(CHUNKS):
+            geno_copy(chunk).start()
 
     def part_copy(k, message):
         if message == tiles + 1:
@@ -143,8 +152,8 @@
             loads[0].wait()
         if t + 1 < tiles:
             loads[t + 1].wait()
-        width = min(2, tiles - t) * TILE
-        product = gram(geno[:, t * TILE : (t + 1) * TILE], geno[:, t * TILE : t * TILE + width])
+        reach = min(t + 2, tiles) * TILE
+        product = gram(geno[:, t * TILE : (t + 1) * TILE], geno[:, t * TILE : reach])
         product = product * (inv_total * LD_SCALE)
         block = product[:, :TILE]
         diag[pl.ds(t, 1), :] = jnp.sum(jnp.where(on_diagonal, block, 0.0), axis=0, keepdims=True)
@@ -159,59 +168,62 @@
         send_part(t)
     send_part(tiles + 1)
 
-    loads[tiles].wait()
-    loads[tiles + 1].wait()
-
-    def place(sweep, slot, value):
+    for copy in loads[tiles:]:
+        copy.wait()
+    everything = slice(0, pieces * width)
+
+    def place(sweep, slot, value, cols=everything):
         high, low = split(value)
-        eff_hi[sweep, slot * TILE : (slot + 1) * TILE] = high
-        eff_lo[sweep, slot * TILE : (slot + 1) * TILE] = low
-
-    def clear(sweep, slot):
-        zero = jnp.zeros((TILE, eff_hi.shape[2]), BF16)
-        eff_hi[sweep, slot * TILE : (slot + 1) * TILE] = zero
-        eff_lo[sweep, slot * TILE : (slot + 1) * TILE] = zero
-
+        eff_hi[sweep, slot * TILE : (slot + 1) * TILE, cols] = high
+        eff_lo[sweep, slot * TILE : (slot + 1) * TILE, cols] = low
+
+    def edge_copy(sweep, side, piece):
+        return pltpu.make_async_remote_copy(
+            src_ref=edge_code.at[sweep, side, piece], dst_ref=edge_got.at[sweep, side, piece],
+            send_sem=edge_send.at[sweep, side, piece], recv_sem=edge_recv.at[sweep, side, piece],
+            device_id={"var": following if side else prev}, device_id_type=MESH,
+        )
+
+    def send_edge(sweep, side, piece):
+        @pl.when(has_next if side else has_prev)
+        def _():
+            edge_copy(sweep, side, piece).start()
+
+    def take_edge(sweep, side, piece):
+        slot = 0 if side else tiles + 1
+        exists = has_prev if side else has_next
+
+        @pl.when(exists)
+        def _():
+            edge_copy(sweep, side, piece).wait_recv()
+            place(sweep, slot, decode(edge_got[sweep, side, piece]), slices[piece])
+
+        @pl.when(jnp.logical_not(exists))
+        def _():
+            place(sweep, slot, jnp.zeros((TILE, width), F32), slices[piece])
+
+    for side, rows in ((1, slice(last * TILE, tiles * TILE)), (0, slice(0, TILE))):
+        for piece in range(pieces):
+            edge_code[0, side, piece] = encode(start[rows, slices[piece]])
+            if side:
+                send_edge(0, side, piece)
     for t in range(tiles):
         place(0, t + 1, start[t * TILE : (t + 1) * TILE])
-    edge_code[0, 0] = encode(start[:TILE])
-    edge_code[0, 1] = encode(start[last * TILE :])
-
-    def edge_copy(sweep, side):
-        return pltpu.make_async_remote_copy(
-            src_ref=edge_code.at[sweep, side], dst_ref=edge_got.at[sweep, side],
-            send_sem=edge_send.at[sweep, side], recv_sem=edge_recv.at[sweep, side],
-            device_id={"var": following if side else prev}, device_id_type=MESH,
-        )
-
-    def send_edge(sweep, side):
-        @pl.when(has_next if side else has_prev)
-        def _():
-            edge_copy(sweep, side).start()
-
-    def take_edge(sweep, side):
-        slot = 0 if side else tiles + 1
-        exists = has_prev if side else has_next
-
-        @pl.when(exists)
-        def _():
-            edge_copy(sweep, side).wait_recv()
-            place(sweep, slot, decode(edge_got[sweep, side]))
-
-        @pl.when(jnp.logical_not(exists))
-        def _():
-            clear(sweep, slot)
 
     @pl.when(has_prev)
     def _():
-        geno_copy.wait_recv()
-        product = gram(halo[...], geno[:, :TILE]) * (inv_total * LD_SCALE)
-        own[cross_at:total_rows] = product
-        code[cross_at:total_rows] = encode(product)
+        crossing = jnp.zeros((TILE, TILE), F32)
+        for chunk in range(CHUNKS):
+            rows = slice(chunk * depth, (chunk + 1) * depth)
+            geno_copy(chunk).wait_recv()
+            if chunk == CHUNKS - 1:
+                for piece in range(pieces):
+                    edge_copy(0, 0, piece).start()
+            crossing = crossing + gram(halo[rows], geno[rows, :TILE])
+        crossing = crossing * (inv_total * LD_SCALE)
+        own[cross_at:total_rows] = crossing
+        code[cross_at:total_rows] = encode(crossing)
         send_part(tiles)
-
-    send_edge(0, 1)
-    send_edge(0, 0)
 
     def summed(begin, size):
         value = own[begin : begin + size]
@@ -243,23 +255,25 @@
             whole = whole + diag_got[k, pl.ds(t, 1), :]
         column = jnp.sum(jnp.where(on_diagonal, whole, 0.0), axis=1, keepdims=True) * (1.0 / LD_SCALE)
         keep.append(1.0 / ((1.0 - shrinkage) * column + shrinkage))
-    limit = limit_ref[...]
-
-    def applied(sweep, tile, first, count):
-        cols = slice(first * TILE, (first + count) * TILE)
+    limit = limit_row[...]
+
+    def applied(sweep, tile, first, count, cols=everything):
+        across = slice(first * TILE, (first + count) * TILE)
         rows = slice((tile + first) * TILE, (tile + first + count) * TILE)
-        high, low = band_hi[tile, :, cols], band_lo[tile, :, cols]
-        near, rest = eff_hi[sweep, rows], eff_lo[sweep, rows]
+        high, low = band_hi[tile, :, across], band_lo[tile, :, across]
+        near, rest = eff_hi[sweep, rows, cols], eff_lo[sweep, rows, cols]
         dot = functools.partial(jnp.dot, preferred_element_type=F32)
         return dot(high, near) + (dot(high, rest) + dot(low, near))
 
-    def finish(tile, combined):
-        adjusted = marg[tile * TILE : (tile + 1) * TILE] - (1.0 - shrinkage) * combined
-        shrunk = adjusted - jnp.clip(adjusted, -limit, limit)
-        return shrunk * keep[tile]
+    def finish(tile, combined, cols=everything):
+        adjusted = marg[tile * TILE : (tile + 1) * TILE, cols] - (1.0 - shrinkage) * combined
+        bound = limit[:, cols]
+        return (adjusted - jnp.clip(adjusted, -bound, bound)) * keep[tile]
 
     for t in range(1, tiles - 1):
         place(1, t + 1, finish(t, applied(0, t, 0, 3)))
+    near_first = applied(0, 0, 1, 2)
+    near_last = applied(0, last, 0, 2)
 
     def back_copy():
         return pltpu.make_async_remote_copy(
@@ -281,11 +295,15 @@
     def _():
         put(0, 0, jnp.zeros((TILE, TILE), F32))
 
-    take_edge(0, 1)
-    value = finish(0, applied(0, 0, 0, 3))
-    edge_code[1, 0] = encode(value)
-    send_edge(1, 0)
-    place(1, 1, value)
+    for piece, cols in enumerate(slices):
+        take_edge(0, 1, piece)
+        value = finish(0, near_first[:, cols] + applied(0, 0, 0, 1, cols), cols)
+        edge_code[1, 0, piece] = encode(value)
+        send_edge(1, 0, piece)
+        place(1, 1, value, cols)
+
+    for piece in range(pieces):
+        take_edge(0, 0, piece)
 
     @pl.when(has_next)
     def _():
@@ -296,32 +314,25 @@
     def _():
         put(last, 2, jnp.zeros((TILE, TILE), F32))
 
-    take_edge(0, 0)
-    value = finish(last, applied(0, last, 0, 3))
-    edge_code[1, 1] = encode(value)
-    send_edge(1, 1)
-    place(1, tiles, value)
-
-    stores = []
-
-    def emit(tile, combined):
-        rows = pl.ds(tile * TILE, TILE)
-        result[tile * TILE : (tile + 1) * TILE] = finish(tile, combined)
-        copy = pltpu.make_async_copy(result.at[rows], out_hbm.at[rows], store_sem.at[tile])
-        copy.start()
-        stores.append(copy)
+    for piece, cols in enumerate(slices):
+        value = finish(last, near_last[:, cols] + applied(0, last, 2, 1, cols), cols)
+        edge_code[1, 1, piece] = encode(value)
+        send_edge(1, 1, piece)
+        place(1, tiles, value, cols)
 
     for t in range(1, tiles - 1):
-        emit(t, applied(1, t, 0, 3))
-    part = applied(1, last, 0, 2)
-    other = applied(1, 0, 1, 2)
-    take_edge(1, 0)
-    emit(last, part + applied(1, last, 2, 1))
-    take_edge(1, 1)
-    emit(0, other + applied(1, 0, 0, 1))
-
-    for copy in stores:
-        copy.wait()
+        out[t * TILE : (t + 1) * TILE] = finish(t, applied(1, t, 0, 3))
+    near_last = applied(1, last, 0, 2)
+    near_first = applied(1, 0, 1, 2)
+    for piece, cols in enumerate(slices):
+        take_edge(1, 0, piece)
+        combined = near_last[:, cols] + applied(1, last, 2, 1, cols)
+        out[last * TILE : tiles * TILE, cols] = finish(last, combined, cols)
+    for piece, cols in enumerate(slices):
+        take_edge(1, 1, piece)
+        combined = near_first[:, cols] + applied(1, 0, 0, 1, cols)
+        out[:TILE, cols] = finish(0, combined, cols)
+
     for k in range(len(peers)):
         for message in list(range(tiles)) + [tiles + 1]:
             part_copy(k, message).wait_send()
@@ -332,13 +343,16 @@
             part_copy(k, tiles).wait_send()
         back_copy().wait_send()
         for sweep in range(SWEEPS):
-            edge_copy(sweep, 0).wait_send()
+            for piece in range(pieces):
+                edge_copy(sweep, 0, piece).wait_send()
 
     @pl.when(has_next)
     def _():
-        geno_copy.wait_send()
+        for chunk in range(CHUNKS):
+            geno_copy(chunk).wait_send()
         for sweep in range(SWEEPS):
-            edge_copy(sweep, 1).wait_send()
+            for piece in range(pieces):
+                edge_copy(sweep, 1, piece).wait_send()
 
 
 def local(genotypes, marginal, start_effects, thresholds):
@@ -348,6 +362,8 @@
     var_size, samp_size = lax.axis_size("var"), lax.axis_size("samp")
     others = samp_size - 1
     rows = tiles * (HALF + TILE)
+    pieces = 2 if traits % 256 == 0 else 1
+    width = traits // pieces
     dma = pltpu.SemaphoreType.DMA
     body = functools.partial(
         kernel, tiles, var_size, samp_size, 1.0 / (samples * samp_size)
@@ -355,13 +371,14 @@
     return pl.pallas_call(
         body,
         out_shape=jax.ShapeDtypeStruct((variants, traits), F32),
-        in_specs=[pl.BlockSpec(memory_space=pl.ANY)] * 3 + [pl.BlockSpec(memory_space=pltpu.VMEM)],
-        out_specs=pl.BlockSpec(memory_space=pl.ANY),
+        in_specs=[pl.BlockSpec(memory_space=pltpu.HBM)] * 4,
+        out_specs=pl.BlockSpec(memory_space=pltpu.VMEM),
         scratch_shapes=[
             pltpu.VMEM((samples, variants), BF16),
             pltpu.VMEM((samples, TILE), BF16),
             pltpu.VMEM((variants, traits), F32),
             pltpu.VMEM((variants, traits), F32),
+            pltpu.VMEM((1, traits), F32),
             pltpu.VMEM((rows, TILE), F32),
             pltpu.VMEM((rows, TILE), BF16),
             pltpu.VMEM((others, rows, TILE), BF16),
@@ -371,24 +388,26 @@
             pltpu.VMEM((tiles, TILE, 3 * TILE), BF16),
             pltpu.VMEM((SWEEPS, (tiles + 2) * TILE, traits), BF16),
             pltpu.VMEM((SWEEPS, (tiles + 2) * TILE, traits), BF16),
-            pltpu.VMEM((SWEEPS, 2, TILE, traits), BF16),
-            pltpu.VMEM((SWEEPS, 2, TILE, traits), BF16),
+            pltpu.VMEM((SWEEPS, 2, pieces, TILE, width), BF16),
+            pltpu.VMEM((SWEEPS, 2, pieces, TILE, width), BF16),
             pltpu.VMEM((TILE, TILE), BF16),
             pltpu.VMEM((TILE, TILE), BF16),
-            pltpu.VMEM((variants, traits), F32),
-            dma((tiles + 2,)),
-            dma((tiles,)),
-            dma((2,)),
+            dma((tiles + 3,)),
+            dma((CHUNKS,)),
+            dma((CHUNKS,)),
             dma((others, tiles + 2)),
             dma((others, tiles + 2)),
             dma((2,)),
-            dma((SWEEPS, 2)),
-            dma((SWEEPS, 2)),
+            dma((SWEEPS, 2, pieces)),
+            dma((SWEEPS, 2, pieces)),
         ],
         compiler_params=pltpu.CompilerParams(
-            collective_id=0, has_side_effects=True, vmem_limit_bytes=60 * 1024 * 1024
+            collective_id=0, has_side_effects=True, vmem_limit_bytes=VMEM_BYTES
         ),
-    )(genotypes, marginal, start_effects, thresholds[None, :])
+    )(*(
+        pltpu.with_memory_space_constraint(array, pltpu.HBM)
+        for array in (genotypes, marginal, start_effects, thresholds[None, :])
+    ))
 
 
 def solution(mesh):

time: 37.2 us -> 32.8 us (0.88)
  the two profiles are of different devices: /device:TPU:8 before, /device:TPU:12 now
where the time goes in v2:
time: 32.8 us; the launch traced here: 32.6 us
  Pallas kernels  31.5 us (96%)
  local copies, waits for them, and re-layouts  1.15 us (4%)
    pallas_call x1, Pallas kernels, local(): pl.pallas_call(body, out_shape=jax.ShapeDtypeStruct((variants, traits), F...  31.5 us
    unnamed x1, local copies, waits for them, and re-layouts  1.15 us

profile of v2, /device:TPU:12, one launch (start us, length us, event | category | flops | bytes accessed | tf_op | source)
XLA Modules:
  0.0 32.6 jit_solution(8505074821703925174)
XLA Ops:
  0.0 31.5 %shard_map.46 = f32[768,512]{1,0:T(8,128)S(1)} custom-call(bf16[2048,768]{1,0:T(8,128)(2,1)} %geno_hbm.1, f32[768,512]{1,0:T(8,128)} %marg_hbm.1, f32[768,512]{1,0:T(8,128)} %start_hbm.1, f32[1,512]{1,0:T(1,128)} %bitcast.1), custom_call_target="tpu_custom_call" | custom-call | tf_op jit(solution)/shard_map/pallas_call | solution.py:371
  31.5 1.1 %copy.6 = f32[768,512]{1,0:T(8,128)} copy(f32[768,512]{1,0:T(8,128)S(1)} %shard_map.46) | data formatting | bytes 3145728

commit v3 on v2

--- a/solution.py
+++ b/solution.py
@@ -11,6 +11,7 @@
 HALF = TILE // 2
 SWEEPS = 2
 CHUNKS = 4
+TINY = 2.0**-126
 VMEM_BYTES = 40 * 1024 * 1024
 LD_SCALE = 1024.0
 
@@ -29,7 +30,9 @@
 
 def decode(code):
     code = code.astype(F32)
-    root = jnp.sqrt(jnp.sqrt(jnp.sqrt(jnp.abs(code))))
+    size = jnp.abs(code)
+    fourth_root = lax.rsqrt(lax.rsqrt(jnp.maximum(size, TINY)))
+    root = jnp.where(size < TINY, 0.0, fourth_root * lax.rsqrt(fourth_root))
     return jnp.where(code < 0, -root, root)
 
 
@@ -165,8 +168,9 @@
             beside = product[:, TILE:]
             own[begin + HALF : begin + step] = beside
             code[begin + HALF : begin + step] = encode(beside)
+        if t == last:
+            send_part(tiles + 1)
         send_part(t)
-    send_part(tiles + 1)
 
     for copy in loads[tiles:]:
         copy.wait()
@@ -209,6 +213,39 @@
                 send_edge(0, side, piece)
     for t in range(tiles):
         place(0, t + 1, start[t * TILE : (t + 1) * TILE])
+
+    def summed(begin, size):
+        value = own[begin : begin + size]
+        for k in range(len(peers)):
+            value = value + decode(got[k, begin : begin + size])
+        return value
+
+    def put(tile, slot, value):
+        high, low = split(value)
+        band_hi[tile, :, slot * TILE : (slot + 1) * TILE] = high
+        band_lo[tile, :, slot * TILE : (slot + 1) * TILE] = low
+
+    def applied(sweep, tile, first, count, cols=everything):
+        across = slice(first * TILE, (first + count) * TILE)
+        rows = slice((tile + first) * TILE, (tile + first + count) * TILE)
+        high, low = band_hi[tile, :, across], band_lo[tile, :, across]
+        near, rest = eff_hi[sweep, rows, cols], eff_lo[sweep, rows, cols]
+        dot = functools.partial(jnp.dot, preferred_element_type=F32)
+        return dot(high, near) + (dot(high, rest) + dot(low, near))
+
+    def add_tile(t):
+        for k in range(len(peers)):
+            part_copy(k, t).wait_recv()
+        begin = t * step
+        put(t, 1, unpack_symmetric(summed(begin, HALF)) * (1.0 / LD_SCALE))
+        if t + 1 < tiles:
+            beside = summed(begin + HALF, TILE) * (1.0 / LD_SCALE)
+            put(t, 2, beside)
+            put(t + 1, 0, beside.T)
+
+    for t in range(last):
+        add_tile(t)
+    near_first = applied(0, 0, 1, 2)
 
     @pl.when(has_prev)
     def _():
@@ -225,29 +262,9 @@
         code[cross_at:total_rows] = encode(crossing)
         send_part(tiles)
 
-    def summed(begin, size):
-        value = own[begin : begin + size]
-        for k in range(len(peers)):
-            value = value + decode(got[k, begin : begin + size])
-        return value
-
-    def put(tile, slot, value):
-        high, low = split(value)
-        band_hi[tile, :, slot * TILE : (slot + 1) * TILE] = high
-        band_lo[tile, :, slot * TILE : (slot + 1) * TILE] = low
-
+    add_tile(last)
     for k in range(len(peers)):
         part_copy(k, tiles + 1).wait_recv()
-    for t in range(tiles):
-        for k in range(len(peers)):
-            part_copy(k, t).wait_recv()
-        begin = t * step
-        put(t, 1, unpack_symmetric(summed(begin, HALF)) * (1.0 / LD_SCALE))
-        if t + 1 < tiles:
-            beside = summed(begin + HALF, TILE) * (1.0 / LD_SCALE)
-            put(t, 2, beside)
-            put(t + 1, 0, beside.T)
-
     keep = []
     for t in range(tiles):
         whole = diag[pl.ds(t, 1), :]
@@ -257,14 +274,6 @@
         keep.append(1.0 / ((1.0 - shrinkage) * column + shrinkage))
     limit = limit_row[...]
 
-    def applied(sweep, tile, first, count, cols=everything):
-        across = slice(first * TILE, (first + count) * TILE)
-        rows = slice((tile + first) * TILE, (tile + first + count) * TILE)
-        high, low = band_hi[tile, :, across], band_lo[tile, :, across]
-        near, rest = eff_hi[sweep, rows, cols], eff_lo[sweep, rows, cols]
-        dot = functools.partial(jnp.dot, preferred_element_type=F32)
-        return dot(high, near) + (dot(high, rest) + dot(low, near))
-
     def finish(tile, combined, cols=everything):
         adjusted = marg[tile * TILE : (tile + 1) * TILE, cols] - (1.0 - shrinkage) * combined
         bound = limit[:, cols]
@@ -272,7 +281,6 @@
 
     for t in range(1, tiles - 1):
         place(1, t + 1, finish(t, applied(0, t, 0, 3)))
-    near_first = applied(0, 0, 1, 2)
     near_last = applied(0, last, 0, 2)
 
     def back_copy():

time: 32.8 us -> 33 us (level); the launches traced: 32.6 us -> 32.4 us
  no operation moved by 1% of the time
where the time goes in v3:
time: 33 us; the launch traced here: 32.4 us
  Pallas kernels  31.3 us (95%)
  local copies, waits for them, and re-layouts  1.15 us (3%)
    pallas_call x1, Pallas kernels, local(): pl.pallas_call(body, out_shape=jax.ShapeDtypeStruct((variants, traits), F...  31.3 us
    unnamed x1, local copies, waits for them, and re-layouts  1.15 us

profile of v3, /device:TPU:12, one launch (start us, length us, event | category | flops | bytes accessed | tf_op | source)
XLA Modules:
  0.0 32.4 jit_solution(2576793955597414031)
XLA Ops:
  0.0 31.3 %shard_map.46 = f32[768,512]{1,0:T(8,128)S(1)} custom-call(bf16[2048,768]{1,0:T(8,128)(2,1)} %geno_hbm.1, f32[768,512]{1,0:T(8,128)} %marg_hbm.1, f32[768,512]{1,0:T(8,128)} %start_hbm.1, f32[1,512]{1,0:T(1,128)} %bitcast.1), custom_call_target="tpu_custom_call" | custom-call | tf_op jit(solution)/shard_map/pallas_call | solution.py:379
  31.3 1.1 %copy.6 = f32[768,512]{1,0:T(8,128)} copy(f32[768,512]{1,0:T(8,128)S(1)} %shard_map.46) | data formatting | bytes 3145728

commit v4 on v3

--- a/solution.py
+++ b/solution.py
@@ -243,25 +243,29 @@
             put(t, 2, beside)
             put(t + 1, 0, beside.T)
 
+    def cross_step(now):
+        @pl.when(jnp.logical_and(has_prev, now))
+        def _():
+            crossing = jnp.zeros((TILE, TILE), F32)
+            for chunk in range(CHUNKS):
+                rows = slice(chunk * depth, (chunk + 1) * depth)
+                geno_copy(chunk).wait_recv()
+                if chunk == CHUNKS - 1:
+                    for piece in range(pieces):
+                        edge_copy(0, 0, piece).start()
+                crossing = crossing + gram(halo[rows], geno[rows, :TILE])
+            crossing = crossing * (inv_total * LD_SCALE)
+            own[cross_at:total_rows] = crossing
+            code[cross_at:total_rows] = encode(crossing)
+            send_part(tiles)
+
+    nearby = lax.rem(var, 2) == 1
+    cross_step(nearby)
     for t in range(last):
         add_tile(t)
     near_first = applied(0, 0, 1, 2)
 
-    @pl.when(has_prev)
-    def _():
-        crossing = jnp.zeros((TILE, TILE), F32)
-        for chunk in range(CHUNKS):
-            rows = slice(chunk * depth, (chunk + 1) * depth)
-            geno_copy(chunk).wait_recv()
-            if chunk == CHUNKS - 1:
-                for piece in range(pieces):
-                    edge_copy(0, 0, piece).start()
-            crossing = crossing + gram(halo[rows], geno[rows, :TILE])
-        crossing = crossing * (inv_total * LD_SCALE)
-        own[cross_at:total_rows] = crossing
-        code[cross_at:total_rows] = encode(crossing)
-        send_part(tiles)
-
+    cross_step(jnp.logical_not(nearby))
     add_tile(last)
     for k in range(len(peers)):
         part_copy(k, tiles + 1).wait_recv()
@@ -370,7 +374,7 @@
     var_size, samp_size = lax.axis_size("var"), lax.axis_size("samp")
     others = samp_size - 1
     rows = tiles * (HALF + TILE)
-    pieces = 2 if traits % 256 == 0 else 1
+    pieces = 1
     width = traits // pieces
     dma = pltpu.SemaphoreType.DMA
     body = functools.partial(

time: 33 us -> 32.7 us (level); the launches traced: 32.4 us -> 32.5 us
  no operation moved by 1% of the time
where the time goes in v4:
time: 32.7 us; the launch traced here: 32.5 us
  Pallas kernels  31.4 us (96%)
  local copies, waits for them, and re-layouts  1.15 us (4%)
    pallas_call x1, Pallas kernels, local(): pl.pallas_call(body, out_shape=jax.ShapeDtypeStruct((variants, traits), F...  31.4 us
    unnamed x1, local copies, waits for them, and re-layouts  1.15 us

profile of v4, /device:TPU:12, one launch (start us, length us, event | category | flops | bytes accessed | tf_op | source)
XLA Modules:
  0.0 32.5 jit_solution(16916876671941277037)
XLA Ops:
  0.0 31.4 %shard_map.46 = f32[768,512]{1,0:T(8,128)S(1)} custom-call(bf16[2048,768]{1,0:T(8,128)(2,1)} %geno_hbm.1, f32[768,512]{1,0:T(8,128)} %marg_hbm.1, f32[768,512]{1,0:T(8,128)} %start_hbm.1, f32[1,512]{1,0:T(1,128)} %bitcast.1), custom_call_target="tpu_custom_call" | custom-call | tf_op jit(solution)/shard_map/pallas_call | solution.py:383
  31.4 1.1 %copy.6 = f32[768,512]{1,0:T(8,128)} copy(f32[768,512]{1,0:T(8,128)S(1)} %shard_map.46) | data formatting | bytes 3145728
